TPU v7x, 256 devices: a whole 4x4x8 slice. The times are simulated.
256 devices in a mesh: row: 16 (over z, core), col: 16 (over x, y).
Axes of the slice: x: 4, y: 4, z: 8, core: 2. Of those that a mesh axis runs over, the one named last changes fastest.
Arguments:
- tensor: float32 [12, 8192, 8192], P(None, 'row', 'col'), may hold values from -6 to 6
- factor_b: float32 [8192, 128], P(('col', 'row')), may hold values from -0.0625 to 0.0625
- factor_c: float32 [12, 128], replicated, may hold values from -1.75 to 1.75
Outputs:
- a_update: float32 [8192, 128], P(('row', 'col'))
- b_update: float32 [8192, 128], P(('col', 'row'))
All inputs are finite; a program needn't handle non-finite values.
Results may differ from a plain program's by a relative error of at most 0.00012.
Values sent between devices are 32-bit elements; how exact they have to be, the bound alone decides.
No kernel may reach another device: no remote copies, remote signals or barrier semaphores. Data moves between devices by JAX's collectives and lax.ppermute only.
A program may use at most 64 MiB of HBM per device.

v0:
```python
import jax
import jax.numpy as jnp
from jax import lax
from jax.sharding import PartitionSpec as P

EPSILON = 1e-06


def solve_system(rhs, system):
    highest = lax.Precision.HIGHEST
    lower = jnp.linalg.cholesky(system)
    inverse = jax.scipy.linalg.cho_solve(
        (lower, True), jnp.eye(system.shape[0], dtype=system.dtype)
    )
    return jnp.dot(rhs, inverse, precision=highest)


def gram_of(matrix):
    return jnp.dot(matrix.T, matrix, precision=lax.Precision.HIGHEST)


def per_device(tensor, factor_b, factor_c):
    highest = lax.Precision.HIGHEST
    rows_block = tensor.shape[1]
    cols_block = tensor.shape[2]
    rank_width = factor_c.shape[1]
    owned_a = rows_block // lax.axis_size("col")
    owned_b = cols_block // lax.axis_size("row")
    c_gram = gram_of(factor_c)
    empty_b = jnp.zeros((cols_block, rank_width), jnp.float32)
    gram_b = lax.psum(gram_of(factor_b), ("row", "col"))
    block = tensor
    khatri = factor_c[:, None, :] * lax.all_gather(factor_b, "row", axis=0, tiled=True)[None, :, :]
    partial_a = jnp.einsum("kij,kjr->ir", block, khatri, precision=highest)
    whole_a = lax.psum(partial_a, "col")
    summed_a = lax.dynamic_slice_in_dim(whole_a, lax.axis_index("col") * owned_a, owned_a, 0)
    a_update = solve_system(summed_a, c_gram * gram_b)
    squares = lax.psum(jnp.sum(a_update * a_update, axis=0), ("row", "col"))
    factor_a = a_update / jnp.sqrt(squares + EPSILON)
    gram_a = lax.psum(gram_of(factor_a), ("row", "col"))
    block = tensor
    khatri = factor_c[:, None, :] * lax.all_gather(factor_a, "col", axis=0, tiled=True)[None, :, :]
    partial_b = empty_b + jnp.einsum("kij,kir->jr", block, khatri, precision=highest)
    whole_b = lax.psum(partial_b, "row")
    summed_b = lax.dynamic_slice_in_dim(whole_b, lax.axis_index("row") * owned_b, owned_b, 0)
    b_update = solve_system(summed_b, c_gram * gram_a)
    return (a_update, b_update)


def solution(mesh):
    placed = (P(None, "row", "col"), P(("col", "row"), None), P())
    return jax.shard_map(
        per_device,
        mesh=mesh,
        in_specs=placed,
        out_specs=(P(("row", "col"), None), P(("col", "row"), None)),
        check_vma=False,
    )
```

profile of v0, /device:TPU:1, one launch (start us, length us, event | category | flops | bytes accessed | tf_op | source)
XLA Modules:
  0.0 809.7 jit_solution(5450451104905007428)
XLA Ops:
  7.2 0.0 all-reduce.7.cloned.1.call-start
  7.2 1.7 fusion.35
  8.9 0.0 all-reduce.7.cloned.1.call-update
  8.9 0.0 all-reduce.5.cloned.1.call-start
  9.0 22.3 %all_gather.6 = f32[512,128]{1,0:T(8,128)S(1)} all-gather(f32[32,128]{1,0:T(8,128)} %param.7), channel_id=1, replica_groups=mesh['row'=16,'col'=16] {'row'}, dimensions={0}, use_global_device_ids=true | all-gather | bytes 278528 | tf_op jit(solution)/shard_map/all_gather | solution.py:33
  31.2 0.0 copy-start
  31.2 18.3 %fusion.8 = f32[512,128]{0,1:T(8,128)} fusion(f32[12,512,512]{2,1,0:T(8,128)} %param.6, f32[512,128]{1,0:T(8,128)S(1)} %all_gather.6, f32[12,128]{1,0:T(8,128)} %param.8), kind=kOutput, calls=%fused_computation.8 | convolution fusion | flops 4832624640 | bytes 13113344 | tf_op jit(solution)/shard_map/kij,kjr->ir/dot_general | solution.py:34
  49.6 0.0 all-reduce.5.cloned.1.call-update
  49.6 0.2 all-reduce.11.cloned.1.call-start
  49.8 209.2 %all-reduce.7.cloned.1.call-done = f32[128,128]{0,1:T(8,128)} async-done(((f32[128,128]{0,1:T(8,128)}), f32[128,128]{0,1:T(8,128)}) %all-reduce.7.cloned.1.call-update) | async-done | bytes 65552 | tf_op jit(solution)/shard_map/psum | solution.py:31
  259.1 0.0 copy-done
  259.1 1.1 fusion.34
  260.2 0.1 copy.7
  260.3 11.7 %cholesky.44 = f32[128,128]{1,0:T(8,128)S(1)} custom-call(f32[128,128]{1,0:T(8,128)S(1)} %fusion.27), custom_call_target="Cholesky" | custom-call | tf_op jit(solution)/shard_map/jit(cholesky)/cholesky | solution.py:11
  272.1 0.6 compare_reduce_fusion.1
  272.7 0.7 fusion.18
  273.4 9.8 %custom-call.8 = f32[1,128,128]{1,2,0:T(8,128)S(1)} custom-call(f32[1,128,128]{2,1,0:T(8,128)S(1)} %fusion.18), custom_call_target="InvertDiagBlocksLowerTriangular" | custom-call | tf_op jit(solution)/shard_map/jit(_cho_solve)/triangular_solve | solution.py:12
  283.2 0.3 fusion.16
  283.5 0.2 fusion.24
  283.7 68.0 %all-reduce.5.cloned.1.call-done = f32[512,128]{0,1:T(8,128)} async-done(((f32[512,128]{0,1:T(8,128)}), f32[512,128]{0,1:T(8,128)}) %all-reduce.5.cloned.1.call-update) | async-done | bytes 262160 | tf_op jit(solution)/shard_map/psum | solution.py:35
  351.7 1.2 multiply_reduce_fusion
  352.8 0.0 copy-start.1
  352.8 77.5 %psum.37 = f32[128]{0:T(128)S(1)} all-reduce(f32[128]{0:T(128)S(1)} %get-tuple-element.6), channel_id=1, replica_groups=mesh['row'=16,'col'=16] {'row','col'}, use_global_device_ids=true, to_apply=%region_5.0 | all-reduce | flops 128 | bytes 1024 | tf_op jit(solution)/shard_map/psum | solution.py:38
  430.3 0.9 fusion.36
  431.3 15.8 %all_gather.7 = f32[512,128]{1,0:T(8,128)S(1)} all-gather(f32[32,128]{1,0:T(8,128)S(1)} %broadcast_divide_fusion), channel_id=1, replica_groups=mesh['row'=16,'col'=16] {'col'}, dimensions={0}, use_global_device_ids=true | all-gather | bytes 278528 | tf_op jit(solution)/shard_map/all_gather | solution.py:42
  447.0 0.0 all-reduce.11.cloned.1.call-update
  447.1 0.3 all-reduce.9.cloned.1.call-start
  447.3 11.4 %fusion.11 = f32[512,128]{0,1:T(8,128)} fusion(f32[12,512,512]{2,1,0:T(8,128)} %param.6, f32[512,128]{1,0:T(8,128)S(1)} %all_gather.7, f32[12,128]{1,0:T(8,128)S(1)} %copy-done), kind=kOutput, calls=%fused_computation.9 | convolution fusion | flops 4832624640 | bytes 13113344 | tf_op jit(solution)/shard_map/kij,kir->jr/dot_general | solution.py:43
  458.7 0.0 copy-done.1
  458.7 0.0 all-reduce.9.cloned.1.call-update
  458.8 234.0 %all-reduce.11.cloned.1.call-done = f32[128,128]{0,1:T(8,128)} async-done(((f32[128,128]{0,1:T(8,128)}), f32[128,128]{0,1:T(8,128)}) %all-reduce.11.cloned.1.call-update) | async-done | bytes 65552 | tf_op jit(solution)/shard_map/psum | solution.py:40
  692.8 0.9 mul.48
  693.7 0.1 copy.10
  693.8 11.7 %cholesky.55 = f32[128,128]{1,0:T(8,128)S(1)} custom-call(f32[128,128]{1,0:T(8,128)S(1)} %fusion.23), custom_call_target="Cholesky" | custom-call | tf_op jit(solution)/shard_map/jit(cholesky)/cholesky | solution.py:11
  705.5 0.6 compare_reduce_fusion
  706.2 0.7 fusion.19
  706.8 9.8 %custom-call.9 = f32[1,128,128]{1,2,0:T(8,128)S(1)} custom-call(f32[1,128,128]{2,1,0:T(8,128)S(1)} %fusion.19), custom_call_target="InvertDiagBlocksLowerTriangular" | custom-call | tf_op jit(solution)/shard_map/jit(_cho_solve)/triangular_solve | solution.py:12
  716.7 0.3 fusion.14
  716.9 0.2 fusion.20
  717.2 84.3 %all-reduce.9.cloned.1.call-done = f32[512,128]{0,1:T(8,128)} async-done(((f32[512,128]{0,1:T(8,128)}), f32[512,128]{0,1:T(8,128)}) %all-reduce.9.cloned.1.call-update) | async-done | bytes 262160 | tf_op jit(solution)/shard_map/psum | solution.py:44
  801.4 1.8 fusion.28
  (6 shorter events, 0.1 us)
Async XLA Ops:
  7.2 251.9 %all-reduce.7.cloned.1.call-start = ((), (), s32[]{:S(2)}) async-start(), calls=%async_computation.1 | async-start | bytes 131072 | tf_op jit(solution)/shard_map/psum | solution.py:31
  8.9 342.7 %all-reduce.5.cloned.1.call-start = ((), (), s32[]{:S(2)}) async-start(), calls=%async_computation | async-start | bytes 524288 | tf_op jit(solution)/shard_map/psum | solution.py:35
  31.2 227.8 %copy-start = (f32[12,128]{1,0:T(8,128)S(1)}, f32[12,128]{1,0:T(8,128)}, u32[]{:S(2)}) copy-start(f32[12,128]{1,0:T(8,128)} %param.8) | copy-start | bytes 18436
  49.6 643.2 %all-reduce.11.cloned.1.call-start = ((), (), s32[]{:S(2)}) async-start(), calls=%async_computation.3 | async-start | bytes 131072 | tf_op jit(solution)/shard_map/psum | solution.py:40
  352.8 105.9 %copy-start.1 = (f32[32,128]{1,0:T(8,128)}, f32[32,128]{1,0:T(8,128)S(1)}, u32[]{:S(2)}) copy-start(f32[32,128]{1,0:T(8,128)S(1)} %get-tuple-element.7) | copy-start | bytes 49156
  447.1 354.4 %all-reduce.9.cloned.1.call-start = ((), (), s32[]{:S(2)}) async-start(), calls=%async_computation.2 | async-start | bytes 524288 | tf_op jit(solution)/shard_map/psum | solution.py:44
Sparse Core Ops, SparseCore 0:
  13.5 245.5 all-reduce.6
  262.2 89.3 all-reduce.4
  447.2 245.5 all-reduce.10
  695.0 106.4 all-reduce.8
where the time goes:
time: 810 us
  waiting for transfers between devices  596 us (74%)
  blocking collectives  116 us (14%)
  other arithmetic  46.6 us (6%)
  matrix products  37.4 us (5%)
  between operations  13.9 us (2%)
    psum x1, waiting for transfers between devices, per_device(): gram_a = lax.psum(gram_of(factor_a), ('row', 'col'))  234 us
    psum x1, waiting for transfers between devices, per_device(): gram_b = lax.psum(gram_of(factor_b), ('row', 'col'))  209 us
    psum x1, waiting for transfers between devices, per_device(): whole_b = lax.psum(partial_b, 'row')  84.3 us
    psum x1, blocking collectives, per_device(): squares = lax.psum(jnp.sum(a_update * a_update, axis=0), ('row', 'col'))  77.5 us
    psum x1, waiting for transfers between devices, per_device(): whole_a = lax.psum(partial_a, 'col')  68 us
    another operation x6, other arithmetic, solve_system(): lower = jnp.linalg.cholesky(system)  24.8 us
    all_gather x1, blocking collectives, per_device(): lax.all_gather(factor_b, 'row', axis=0, tiled=True)[None, :, :]  22.3 us
    another operation x4, other arithmetic, solve_system(): jax.scipy.linalg.cho_solve((lower, True), jnp.eye(system.shape[0], dtype=...  20.9 us
  transfers between devices with their start and end apart: 4, of which 4 were waited for; matrix products, arithmetic and copies ran while one was open for 10% of the time, Pallas kernels for 0%

commit v1 on v0

--- a/solution.py
+++ b/solution.py
@@ -28,7 +28,8 @@
     owned_b = cols_block // lax.axis_size("row")
     c_gram = gram_of(factor_c)
     empty_b = jnp.zeros((cols_block, rank_width), jnp.float32)
-    gram_b = lax.psum(gram_of(factor_b), ("row", "col"))
+    partial = lax.psum(gram_of(factor_b), "row")
+    gram_b = lax.psum(partial, "col")
     block = tensor
     khatri = factor_c[:, None, :] * lax.all_gather(factor_b, "row", axis=0, tiled=True)[None, :, :]
     partial_a = jnp.einsum("kij,kjr->ir", block, khatri, precision=highest)

time: 810 us -> 692 us (0.85)
  waiting for transfers between devices: 596 us -> 477 us
    psum x2, waiting for transfers between devices: 277 us -> 159 us  [the longest x1 93.7 us: per_device(): gram_b = lax.psum(partial, 'col')]
  transfers between devices with their start and end apart: 4 -> 4, of which waited for: 4 -> 4; matrix products, arithmetic and copies ran while one was open for 10% -> 8% of each run, Pallas kernels for 0% -> 0%
where the time goes in v1:
time: 692 us
  waiting for transfers between devices  477 us (69%)
  blocking collectives  116 us (17%)
  other arithmetic  46.6 us (7%)
  matrix products  37.5 us (5%)
  between operations  13.9 us (2%)
    psum x1, waiting for transfers between devices, per_device(): gram_a = lax.psum(gram_of(factor_a), ('row', 'col'))  234 us
    psum x1, waiting for transfers between devices, per_device(): gram_b = lax.psum(partial, 'col')  93.7 us
    psum x1, waiting for transfers between devices, per_device(): whole_b = lax.psum(partial_b, 'row')  84.3 us
    psum x1, blocking collectives, per_device(): squares = lax.psum(jnp.sum(a_update * a_update, axis=0), ('row', 'col'))  77.5 us
    psum x1, waiting for transfers between devices, per_device(): partial = lax.psum(gram_of(factor_b), 'row')  65.4 us
    another operation x6, other arithmetic, solve_system(): lower = jnp.linalg.cholesky(system)  24.8 us
    all_gather x1, blocking collectives, per_device(): lax.all_gather(factor_b, 'row', axis=0, tiled=True)[None, :, :]  22.3 us
    another operation x4, other arithmetic, solve_system(): jax.scipy.linalg.cho_solve((lower, True), jnp.eye(system.shape[0], dtype=...  20.9 us
  transfers between devices with their start and end apart: 4, of which 4 were waited for; matrix products, arithmetic and copies ran while one was open for 8% of the time, Pallas kernels for 0%

profile of v1, /device:TPU:1, one launch (start us, length us, event | category | flops | bytes accessed | tf_op | source)
XLA Modules:
  0.0 691.6 jit_solution(11037113532238475073)
XLA Ops:
  7.2 0.0 all-reduce.6.cloned.1.call-start
  7.2 1.7 fusion.35
  8.9 0.0 all-reduce.6.cloned.1.call-update
  8.9 0.0 all-reduce.12.cloned.1.call-start
  9.0 22.3 %all_gather.6 = f32[512,128]{1,0:T(8,128)S(1)} all-gather(f32[32,128]{1,0:T(8,128)} %param.7), channel_id=1, replica_groups=mesh['row'=16,'col'=16] {'row'}, dimensions={0}, use_global_device_ids=true | all-gather | bytes 278528 | tf_op jit(solution)/shard_map/all_gather | solution.py:34
  31.2 0.0 copy-start
  31.2 18.3 %fusion.8 = f32[512,128]{0,1:T(8,128)} fusion(f32[12,512,512]{2,1,0:T(8,128)} %param.6, f32[512,128]{1,0:T(8,128)S(1)} %all_gather.6, f32[12,128]{1,0:T(8,128)} %param.8), kind=kOutput, calls=%fused_computation.8 | convolution fusion | flops 4832624640 | bytes 13113344 | tf_op jit(solution)/shard_map/kij,kjr->ir/dot_general | solution.py:35
  49.6 65.4 %all-reduce.6.cloned.1.call-done = f32[128,128]{0,1:T(8,128)} async-done(((f32[128,128]{0,1:T(8,128)}), f32[128,128]{0,1:T(8,128)}) %all-reduce.6.cloned.1.call-update) | async-done | bytes 65552 | tf_op jit(solution)/shard_map/psum | solution.py:31
  114.9 0.0 all-reduce.12.cloned.1.call-update
  115.0 0.2 all-reduce.10.cloned.1.call-start
  115.2 93.7 %all-reduce.12.cloned.1.call-done = (f32[128,128]{0,1:T(8,128)}, f32[512,128]{0,1:T(8,128)}) async-done(((f32[128,128]{0,1:T(8,128)}, f32[512,128]{0,1:T(8,128)}), (f32[128,128]{0,1:T(8,128)}, f32[512,128]{0,1:T(8,128)})) %all-reduce.12.cloned.1.call-update) | async-done | bytes 327696 | tf_op jit(solution)/shard_map/psum | solution.py:32
  208.9 0.0 copy-done
  208.9 1.1 fusion.34
  210.0 0.1 copy.7
  210.1 11.7 %cholesky.44 = f32[128,128]{1,0:T(8,128)S(1)} custom-call(f32[128,128]{1,0:T(8,128)S(1)} %fusion.27), custom_call_target="Cholesky" | custom-call | tf_op jit(solution)/shard_map/jit(cholesky)/cholesky | solution.py:11
  221.9 0.6 compare_reduce_fusion.1
  222.5 0.7 fusion.18
  223.2 9.8 %custom-call.8 = f32[1,128,128]{1,2,0:T(8,128)S(1)} custom-call(f32[1,128,128]{2,1,0:T(8,128)S(1)} %fusion.18), custom_call_target="InvertDiagBlocksLowerTriangular" | custom-call | tf_op jit(solution)/shard_map/jit(_cho_solve)/triangular_solve | solution.py:12
  233.0 0.3 fusion.16
  233.3 0.2 fusion.24
  233.5 1.2 multiply_reduce_fusion
  234.7 0.0 copy-start.1
  234.7 77.5 %psum.45 = f32[128]{0:T(128)S(1)} all-reduce(f32[128]{0:T(128)S(1)} %get-tuple-element.8), channel_id=1, replica_groups=mesh['row'=16,'col'=16] {'row','col'}, use_global_device_ids=true, to_apply=%region_6.0 | all-reduce | flops 128 | bytes 1024 | tf_op jit(solution)/shard_map/psum | solution.py:39
  312.2 0.9 fusion.36
  313.1 15.8 %all_gather.7 = f32[512,128]{1,0:T(8,128)S(1)} all-gather(f32[32,128]{1,0:T(8,128)S(1)} %broadcast_divide_fusion), channel_id=1, replica_groups=mesh['row'=16,'col'=16] {'col'}, dimensions={0}, use_global_device_ids=true | all-gather | bytes 278528 | tf_op jit(solution)/shard_map/all_gather | solution.py:43
  328.9 0.0 all-reduce.10.cloned.1.call-update
  328.9 0.3 all-reduce.8.cloned.1.call-start
  329.2 11.4 %fusion.11 = f32[512,128]{0,1:T(8,128)} fusion(f32[12,512,512]{2,1,0:T(8,128)} %param.6, f32[512,128]{1,0:T(8,128)S(1)} %all_gather.7, f32[12,128]{1,0:T(8,128)S(1)} %copy-done), kind=kOutput, calls=%fused_computation.9 | convolution fusion | flops 4832624640 | bytes 13113344 | tf_op jit(solution)/shard_map/kij,kir->jr/dot_general | solution.py:44
  340.6 0.0 copy-done.1
  340.7 0.0 all-reduce.8.cloned.1.call-update
  340.7 234.0 %all-reduce.10.cloned.1.call-done = f32[128,128]{0,1:T(8,128)} async-done(((f32[128,128]{0,1:T(8,128)}), f32[128,128]{0,1:T(8,128)}) %all-reduce.10.cloned.1.call-update) | async-done | bytes 65552 | tf_op jit(solution)/shard_map/psum | solution.py:41
  574.7 0.8 mul.48
  575.5 0.1 copy.10
  575.6 11.7 %cholesky.55 = f32[128,128]{1,0:T(8,128)S(1)} custom-call(f32[128,128]{1,0:T(8,128)S(1)} %fusion.23), custom_call_target="Cholesky" | custom-call | tf_op jit(solution)/shard_map/jit(cholesky)/cholesky | solution.py:11
  587.4 0.6 compare_reduce_fusion
  588.0 0.7 fusion.19
  588.7 9.8 %custom-call.9 = f32[1,128,128]{1,2,0:T(8,128)S(1)} custom-call(f32[1,128,128]{2,1,0:T(8,128)S(1)} %fusion.19), custom_call_target="InvertDiagBlocksLowerTriangular" | custom-call | tf_op jit(solution)/shard_map/jit(_cho_solve)/triangular_solve | solution.py:12
  598.5 0.3 fusion.14
  598.8 0.2 fusion.20
  599.0 84.3 %all-reduce.8.cloned.1.call-done = f32[512,128]{0,1:T(8,128)} async-done(((f32[512,128]{0,1:T(8,128)}), f32[512,128]{0,1:T(8,128)}) %all-reduce.8.cloned.1.call-update) | async-done | bytes 262160 | tf_op jit(solution)/shard_map/psum | solution.py:45
  683.3 1.8 fusion.28
  (6 shorter events, 0.1 us)
Async XLA Ops:
  7.2 107.8 %all-reduce.6.cloned.1.call-start = ((), (), s32[]{:S(2)}) async-start(), calls=%async_computation | async-start | bytes 131072 | tf_op jit(solution)/shard_map/psum | solution.py:31
  8.9 199.9 %all-reduce.12.cloned.1.call-start = ((), (), s32[]{:S(2)}) async-start(), calls=%async_computation.3 | async-start | bytes 655360 | tf_op jit(solution)/shard_map/psum | solution.py:32
  31.2 177.6 %copy-start = (f32[12,128]{1,0:T(8,128)S(1)}, f32[12,128]{1,0:T(8,128)}, u32[]{:S(2)}) copy-start(f32[12,128]{1,0:T(8,128)} %param.8) | copy-start | bytes 18436
  115.0 459.7 %all-reduce.10.cloned.1.call-start = ((), (), s32[]{:S(2)}) async-start(), calls=%async_computation.2 | async-start | bytes 131072 | tf_op jit(solution)/shard_map/psum | solution.py:41
  234.7 106.0 %copy-start.1 = (f32[32,128]{1,0:T(8,128)}, f32[32,128]{1,0:T(8,128)S(1)}, u32[]{:S(2)}) copy-start(f32[32,128]{1,0:T(8,128)S(1)} %get-tuple-element.9) | copy-start | bytes 49156
  328.9 354.4 %all-reduce.8.cloned.1.call-start = ((), (), s32[]{:S(2)}) async-start(), calls=%async_computation.1 | async-start | bytes 524288 | tf_op jit(solution)/shard_map/psum | solution.py:45
Sparse Core Ops, SparseCore 0:
  10.3 104.6 all-reduce.5
  118.2 90.5 all-reduce.11
  329.1 245.5 all-reduce.9
  576.8 106.3 all-reduce.7

commit v2 on v0

--- a/solution.py
+++ b/solution.py
@@ -37,7 +37,9 @@
     a_update = solve_system(summed_a, c_gram * gram_b)
     squares = lax.psum(jnp.sum(a_update * a_update, axis=0), ("row", "col"))
     factor_a = a_update / jnp.sqrt(squares + EPSILON)
-    gram_a = lax.psum(gram_of(factor_a), ("row", "col"))
+    gram_a = gram_of(factor_a)
+    for mesh_axis in ("col", "row"):
+        gram_a = lax.psum(gram_a, mesh_axis)
     block = tensor
     khatri = factor_c[:, None, :] * lax.all_gather(factor_a, "col", axis=0, tiled=True)[None, :, :]
     partial_b = empty_b + jnp.einsum("kij,kir->jr", block, khatri, precision=highest)

time: 810 us -> 686 us (0.85)
  waiting for transfers between devices: 596 us -> 472 us
    psum x2, waiting for transfers between devices: 318 us -> 194 us  [per_device(): gram_a = lax.psum(gram_a, mesh_axis)]
  transfers between devices with their start and end apart: 4 -> 4, of which waited for: 4 -> 4; matrix products, arithmetic and copies ran while one was open for 10% -> 8% of each run, Pallas kernels for 0% -> 0%
where the time goes in v2:
time: 686 us
  waiting for transfers between devices  472 us (69%)
  blocking collectives  116 us (17%)
  other arithmetic  46.6 us (7%)
  matrix products  37.5 us (5%)
  between operations  13.9 us (2%)
    psum x1, waiting for transfers between devices, per_device(): gram_b = lax.psum(gram_of(factor_b), ('row', 'col'))  209 us
    psum x2, waiting for transfers between devices, per_device(): gram_a = lax.psum(gram_a, mesh_axis)  194 us
    psum x1, blocking collectives, per_device(): squares = lax.psum(jnp.sum(a_update * a_update, axis=0), ('row', 'col'))  77.5 us
    psum x1, waiting for transfers between devices, per_device(): whole_a = lax.psum(partial_a, 'col')  68 us
    another operation x6, other arithmetic, solve_system(): lower = jnp.linalg.cholesky(system)  24.8 us
    all_gather x1, blocking collectives, per_device(): lax.all_gather(factor_b, 'row', axis=0, tiled=True)[None, :, :]  22.3 us
    another operation x4, other arithmetic, solve_system(): jax.scipy.linalg.cho_solve((lower, True), jnp.eye(system.shape[0], dtype=...  20.9 us
    dot_general x1, matrix products, per_device(): partial_a = jnp.einsum('kij,kjr->ir', block, khatri, precision=highest)  18.3 us
  transfers between devices with their start and end apart: 4, of which 4 were waited for; matrix products, arithmetic and copies ran while one was open for 8% of the time, Pallas kernels for 0%

profile of v2, /device:TPU:1, one launch (start us, length us, event | category | flops | bytes accessed | tf_op | source)
XLA Modules:
  0.0 685.9 jit_solution(141782250365787634)
XLA Ops:
  7.2 0.0 all-reduce.8.cloned.1.call-start
  7.2 1.7 fusion.35
  8.9 0.0 all-reduce.8.cloned.1.call-update
  8.9 0.0 all-reduce.6.cloned.1.call-start
  9.0 22.3 %all_gather.6 = f32[512,128]{1,0:T(8,128)S(1)} all-gather(f32[32,128]{1,0:T(8,128)} %param.7), channel_id=1, replica_groups=mesh['row'=16,'col'=16] {'row'}, dimensions={0}, use_global_device_ids=true | all-gather | bytes 278528 | tf_op jit(solution)/shard_map/all_gather | solution.py:33
  31.2 0.0 copy-start
  31.2 18.3 %fusion.8 = f32[512,128]{0,1:T(8,128)} fusion(f32[12,512,512]{2,1,0:T(8,128)} %param.6, f32[512,128]{1,0:T(8,128)S(1)} %all_gather.6, f32[12,128]{1,0:T(8,128)} %param.8), kind=kOutput, calls=%fused_computation.8 | convolution fusion | flops 4832624640 | bytes 13113344 | tf_op jit(solution)/shard_map/kij,kjr->ir/dot_general | solution.py:34
  49.6 0.0 all-reduce.6.cloned.1.call-update
  49.6 0.2 all-reduce.10.cloned.1.call-start
  49.9 209.2 %all-reduce.8.cloned.1.call-done = f32[128,128]{0,1:T(8,128)} async-done(((f32[128,128]{0,1:T(8,128)}), f32[128,128]{0,1:T(8,128)}) %all-reduce.8.cloned.1.call-update) | async-done | bytes 65552 | tf_op jit(solution)/shard_map/psum | solution.py:31
  259.1 0.0 copy-done
  259.1 1.1 fusion.34
  260.2 0.1 copy.7
  260.3 11.7 %cholesky.44 = f32[128,128]{1,0:T(8,128)S(1)} custom-call(f32[128,128]{1,0:T(8,128)S(1)} %fusion.27), custom_call_target="Cholesky" | custom-call | tf_op jit(solution)/shard_map/jit(cholesky)/cholesky | solution.py:11
  272.1 0.6 compare_reduce_fusion.1
  272.7 0.7 fusion.18
  273.4 9.8 %custom-call.8 = f32[1,128,128]{1,2,0:T(8,128)S(1)} custom-call(f32[1,128,128]{2,1,0:T(8,128)S(1)} %fusion.18), custom_call_target="InvertDiagBlocksLowerTriangular" | custom-call | tf_op jit(solution)/shard_map/jit(_cho_solve)/triangular_solve | solution.py:12
  283.2 0.3 fusion.16
  283.5 0.2 fusion.24
  283.7 68.0 %all-reduce.6.cloned.1.call-done = f32[512,128]{0,1:T(8,128)} async-done(((f32[512,128]{0,1:T(8,128)}), f32[512,128]{0,1:T(8,128)}) %all-reduce.6.cloned.1.call-update) | async-done | bytes 262160 | tf_op jit(solution)/shard_map/psum | solution.py:35
  351.7 1.2 multiply_reduce_fusion
  352.8 0.0 copy-start.1
  352.8 77.5 %psum.44 = f32[128]{0:T(128)S(1)} all-reduce(f32[128]{0:T(128)S(1)} %get-tuple-element.8), channel_id=1, replica_groups=mesh['row'=16,'col'=16] {'row','col'}, use_global_device_ids=true, to_apply=%region_5.0 | all-reduce | flops 128 | bytes 1024 | tf_op jit(solution)/shard_map/psum | solution.py:38
  430.3 0.9 fusion.36
  431.2 15.8 %all_gather.7 = f32[512,128]{1,0:T(8,128)S(1)} all-gather(f32[32,128]{1,0:T(8,128)S(1)} %broadcast_divide_fusion), channel_id=1, replica_groups=mesh['row'=16,'col'=16] {'col'}, dimensions={0}, use_global_device_ids=true | all-gather | bytes 278528 | tf_op jit(solution)/shard_map/all_gather | solution.py:44
  447.0 0.0 all-reduce.10.cloned.1.call-update
  447.1 0.3 all-reduce.12.cloned.1.call-start
  447.3 11.4 %fusion.11 = f32[512,128]{0,1:T(8,128)} fusion(f32[12,512,512]{2,1,0:T(8,128)} %param.6, f32[512,128]{1,0:T(8,128)S(1)} %all_gather.7, f32[12,128]{1,0:T(8,128)S(1)} %copy-done), kind=kOutput, calls=%fused_computation.9 | convolution fusion | flops 4832624640 | bytes 13113344 | tf_op jit(solution)/shard_map/kij,kir->jr/dot_general | solution.py:45
  458.8 0.0 copy-done.1
  458.8 82.5 %all-reduce.10.cloned.1.call-done = f32[128,128]{0,1:T(8,128)} async-done(((f32[128,128]{0,1:T(8,128)}), f32[128,128]{0,1:T(8,128)}) %all-reduce.10.cloned.1.call-update) | async-done | bytes 65552 | tf_op jit(solution)/shard_map/psum | solution.py:42
  541.3 0.0 all-reduce.12.cloned.1.call-update
  541.4 111.9 %all-reduce.12.cloned.1.call-done = (f32[128,128]{0,1:T(8,128)}, f32[512,128]{0,1:T(8,128)}) async-done(((f32[128,128]{0,1:T(8,128)}, f32[512,128]{0,1:T(8,128)}), (f32[128,128]{0,1:T(8,128)}, f32[512,128]{0,1:T(8,128)})) %all-reduce.12.cloned.1.call-update) | async-done | bytes 327696 | tf_op jit(solution)/shard_map/psum | solution.py:42
  653.2 0.8 mul.48
  654.1 0.1 copy.10
  654.2 11.7 %cholesky.55 = f32[128,128]{1,0:T(8,128)S(1)} custom-call(f32[128,128]{1,0:T(8,128)S(1)} %fusion.23), custom_call_target="Cholesky" | custom-call | tf_op jit(solution)/shard_map/jit(cholesky)/cholesky | solution.py:11
  665.9 0.6 compare_reduce_fusion
  666.6 0.7 fusion.19
  667.2 9.8 %custom-call.9 = f32[1,128,128]{1,2,0:T(8,128)S(1)} custom-call(f32[1,128,128]{2,1,0:T(8,128)S(1)} %fusion.19), custom_call_target="InvertDiagBlocksLowerTriangular" | custom-call | tf_op jit(solution)/shard_map/jit(_cho_solve)/triangular_solve | solution.py:12
  677.1 0.3 fusion.14
  677.4 0.2 fusion.20
  677.6 1.8 fusion.28
  (6 shorter events, 0.1 us)
Async XLA Ops:
  7.2 251.9 %all-reduce.8.cloned.1.call-start = ((), (), s32[]{:S(2)}) async-start(), calls=%async_computation.1 | async-start | bytes 131072 | tf_op jit(solution)/shard_map/psum | solution.py:31
  8.9 342.7 %all-reduce.6.cloned.1.call-start = ((), (), s32[]{:S(2)}) async-start(), calls=%async_computation | async-start | bytes 524288 | tf_op jit(solution)/shard_map/psum | solution.py:35
  31.2 227.8 %copy-start = (f32[12,128]{1,0:T(8,128)S(1)}, f32[12,128]{1,0:T(8,128)}, u32[]{:S(2)}) copy-start(f32[12,128]{1,0:T(8,128)} %param.8) | copy-start | bytes 18436
  49.6 491.7 %all-reduce.10.cloned.1.call-start = ((), (), s32[]{:S(2)}) async-start(), calls=%async_computation.2 | async-start | bytes 131072 | tf_op jit(solution)/shard_map/psum | solution.py:42
  352.8 105.9 %copy-start.1 = (f32[32,128]{1,0:T(8,128)}, f32[32,128]{1,0:T(8,128)S(1)}, u32[]{:S(2)}) copy-start(f32[32,128]{1,0:T(8,128)S(1)} %get-tuple-element.9) | copy-start | bytes 49156
  447.1 206.2 %all-reduce.12.cloned.1.call-start = ((), (), s32[]{:S(2)}) async-start(), calls=%async_computation.3 | async-start | bytes 655360 | tf_op jit(solution)/shard_map/psum | solution.py:42
Sparse Core Ops, SparseCore 0:
  13.5 245.5 all-reduce.7
  262.2 89.3 all-reduce.5
  447.2 94.0 all-reduce.9
  543.6 109.5 all-reduce.11
